TPU v7x, 32 devices: a whole 2x2x4 slice. The times are simulated.
32 devices in a mesh: seq: 4 (over z), tensor: 2 (over y), section: 4 (over x, core).
Axes of the slice: x: 2, y: 2, z: 4, core: 2. Of those that a mesh axis runs over, the one named last changes fastest.
Arguments:
- dec_inputs: bfloat16 [4, 1024, 4096], P('section', 'seq'), may hold values from -64 to 64
- w_query: bfloat16 [4, 4096, 512], P('section', None, 'tensor')
- w_key: bfloat16 [4, 4096, 512], P('section', None, 'tensor')
- w_value: bfloat16 [4, 4096, 512], P('section', None, 'tensor'), may hold values from -0.09375 to 0.09375
- ctx_grad: bfloat16 [4, 1024, 512], P('section', 'seq', 'tensor'), may hold values from -96 to 96
- encoded: bfloat16 [448, 4096], P('seq'), may hold values from -11 to 11
- enc_lengths: int32 [4], replicated, may hold values from 0 to 112, as said below
Outputs:
- dec_grad: bfloat16 [4, 1024, 4096], P('section', 'seq', 'tensor')
- enc_grad: bfloat16 [448, 4096], P('seq', ('tensor', 'section'))
Inputs may be any that keep to these rules, and one draw needn't show every extreme that they name: `enc_lengths`: each block holds a prefix of valid tokens; in every draw some block is wholly valid and blocks may be empty.
All inputs are finite; a program needn't handle non-finite values.
Results may differ from a plain program's by a relative error of at most 0.018.
Values may be sent and summed in bfloat16 or wider, within the bound.
A program may use at most 64 MiB of HBM per device.

v0:
```python
import math
import jax
import jax.numpy as jnp
from jax import lax
from jax.sharding import PartitionSpec as P

masked_fill = -1e30


def body(dec_inputs, w_query, w_key, w_value, ctx_grad, encoded, enc_lengths):
    inputs = dec_inputs[0]
    wq_own = w_query[0]
    wk_own = w_key[0]
    wv_own = w_value[0]
    dout = ctx_grad[0]
    scale = 1.0 / math.sqrt(wq_own.shape[1])
    blocks = enc_lengths.shape[0]
    kdev = encoded.shape[0]
    query = jnp.dot(inputs, wq_own, preferred_element_type=jnp.float32).astype(jnp.bfloat16)
    key = jnp.dot(encoded, wk_own, preferred_element_type=jnp.float32).astype(jnp.bfloat16)
    value = jnp.dot(encoded, wv_own, preferred_element_type=jnp.float32).astype(jnp.bfloat16)
    key_all, value_all = (
        lax.all_gather(key, "seq", axis=0, tiled=True),
        lax.all_gather(value, "seq", axis=0, tiled=True),
    )
    limit = jnp.broadcast_to(enc_lengths[:, None], (blocks, kdev)).reshape(-1)
    slots = lax.broadcasted_iota(jnp.int32, (blocks, kdev), 1).reshape(-1)
    valid = (slots < limit)[None, :]
    scores = jnp.einsum("qd,kd->qk", query, key_all, preferred_element_type=jnp.float32) * scale
    scores = jnp.where(valid, scores, masked_fill)
    top = jnp.max(scores, axis=1, keepdims=True)
    expd = jnp.where(valid, jnp.exp(scores - top), 0.0)
    probs = expd / jnp.sum(expd, axis=1, keepdims=True)
    dprob = jnp.einsum("qd,kd->qk", dout, value_all, preferred_element_type=jnp.float32)
    delta = jnp.sum(probs * dprob, axis=1, keepdims=True)
    dscore = (probs * (dprob - delta) * scale).astype(jnp.bfloat16)
    probs_b = probs.astype(jnp.bfloat16)
    dquery = jnp.dot(dscore, key_all, preferred_element_type=jnp.float32).astype(jnp.bfloat16)
    dkey_part = jnp.einsum("qk,qd->kd", dscore, query, preferred_element_type=jnp.float32)
    dvalue_part = jnp.einsum("qk,qd->kd", probs_b, dout, preferred_element_type=jnp.float32)
    dkey_sum, dvalue_sum = (
        lax.psum_scatter(
            dkey_part.astype(jnp.bfloat16), "seq", scatter_dimension=0, tiled=True
        ).astype(jnp.float32),
        lax.psum_scatter(
            dvalue_part.astype(jnp.bfloat16), "seq", scatter_dimension=0, tiled=True
        ).astype(jnp.float32),
    )
    dkey = dkey_sum.astype(jnp.bfloat16)
    dvalue = dvalue_sum.astype(jnp.bfloat16)
    input_term = jnp.einsum("qd,ed->qe", dquery, wq_own, preferred_element_type=jnp.float32)
    dec_grad = lax.psum_scatter(
        input_term.astype(jnp.bfloat16), "tensor", scatter_dimension=1, tiled=True
    )
    encoder_term = jnp.einsum("kd,ed->ke", dkey, wk_own, preferred_element_type=jnp.float32)
    encoder_term = encoder_term + jnp.einsum(
        "kd,ed->ke", dvalue, wv_own, preferred_element_type=jnp.float32
    )
    enc_grad = lax.psum_scatter(
        encoder_term.astype(jnp.bfloat16), ("tensor", "section"), scatter_dimension=1, tiled=True
    )
    return (dec_grad[None, :, :], enc_grad)


def solution(mesh):
    in_specs = (
        P("section", "seq", None),
        P("section", None, "tensor"),
        P("section", None, "tensor"),
        P("section", None, "tensor"),
        P("section", "seq", "tensor"),
        P("seq", None),
        P(),
    )
    out_specs = (P("section", "seq", "tensor"), P("seq", ("tensor", "section")))
    return jax.shard_map(body, mesh=mesh, in_specs=in_specs, out_specs=out_specs, check_vma=False)
```

profile of v0, /device:TPU:0, one launch (start us, length us, event | category | flops | bytes accessed | tf_op | source)
XLA Modules:
  0.0 163.3 jit_solution(12802926421233766787)
XLA Ops:
  7.2 0.0 reduce-scatter.7.cloned.1.call-start
  7.2 0.9 iota_compare_fusion
  8.1 0.1 lt.11
  8.2 2.5 %fusion.18 = bf16[112,256]{1,0:T(8,128)(2,1)S(1)} fusion(bf16[112,4096]{1,0:T(8,128)(2,1)} %param.12, bf16[1,4096,256]{2,1,0:T(8,128)(2,1)} %param.9), kind=kOutput, calls=%fused_computation.21 | convolution fusion | flops 234909696 | bytes 3072000 | tf_op jit(solution)/shard_map/dot_general | solution.py:20
  10.7 15.6 %all_gather.6 = bf16[448,256]{1,0:T(8,128)(2,1)S(1)} all-gather(bf16[112,256]{1,0:T(8,128)(2,1)S(1)} %fusion.18), channel_id=1, replica_groups=mesh['seq'=4,'tensor'=2,'section'=4] {'seq'}, dimensions={0}, use_global_device_ids=true | all-gather | bytes 286720 | tf_op jit(solution)/shard_map/all_gather | solution.py:23
  26.4 0.4 fusion.21
  26.8 14.2 %all_gather.7 = bf16[448,256]{1,0:T(8,128)(2,1)S(1)} all-gather(bf16[112,256]{1,0:T(8,128)(2,1)S(1)} %fusion.21), channel_id=1, replica_groups=mesh['seq'=4,'tensor'=2,'section'=4] {'seq'}, dimensions={0}, use_global_device_ids=true | all-gather | bytes 286720 | tf_op jit(solution)/shard_map/all_gather | solution.py:24
  41.0 0.7 fusion.13
  41.7 0.3 fusion.30
  42.0 0.1 fusion.25
  42.2 0.3 multiply_reduce_fusion
  42.5 0.2 multiply_convert_fusion
  42.7 0.9 convolution_convert_fusion.2
  43.6 0.0 reduce-scatter.9.cloned.1.call-start
  43.7 1.0 convolution_convert_fusion.1
  44.6 0.0 reduce-scatter.11.cloned.1.call-start
  44.7 19.7 %reduce-scatter.7.cloned.1.call-done = bf16[112,256]{1,0:T(8,128)(2,1)} async-done(((bf16[448,256]{1,0:T(8,128)(2,1)}), bf16[112,256]{1,0:T(8,128)(2,1)}) %reduce-scatter.7.cloned.1.call-update) | async-done | bytes 57360 | tf_op jit(solution)/shard_map/reduce_scatter | solution.py:42
  64.4 3.7 %fusion.4 = f32[112,4096]{1,0:T(8,128)} fusion(bf16[112,256]{1,0:T(8,128)(2,1)} %reduce-scatter.7.cloned.1.call-done, bf16[1,4096,256]{2,1,0:T(8,128)(2,1)} %param.9), kind=kOutput, calls=%fused_computation.6 | convolution fusion | flops 234881024 | bytes 3989504 | tf_op jit(solution)/shard_map/kd,ed->ke/dot_general | solution.py:55
  68.1 16.5 %reduce-scatter.9.cloned.1.call-done = bf16[112,256]{1,0:T(8,128)(2,1)} async-done(((bf16[448,256]{1,0:T(8,128)(2,1)}), bf16[112,256]{1,0:T(8,128)(2,1)}) %reduce-scatter.9.cloned.1.call-update) | async-done | bytes 57360 | tf_op jit(solution)/shard_map/reduce_scatter | solution.py:45
  84.6 3.9 %fusion = bf16[112,4096]{1,0:T(8,128)(2,1)} fusion(f32[112,4096]{1,0:T(8,128)} %fusion.4, bf16[112,256]{1,0:T(8,128)(2,1)} %reduce-scatter.9.cloned.1.call-done, bf16[1,4096,256]{2,1,0:T(8,128)(2,1)} %param.10), kind=kOutput, calls=%fused_computation.2 | convolution fusion | flops 235798528 | bytes 4907008 | tf_op jit(solution)/shard_map/kd,ed->ke/dot_general | solution.py:56
  88.5 0.0 reduce-scatter.5.cloned.1.call-start
  88.5 2.3 %convolution_convert_fusion = bf16[256,4096]{1,0:T(8,128)(2,1)} fusion(bf16[1,4096,256]{2,1,0:T(8,128)(2,1)S(1)} %copy-done, bf16[256,448]{0,1:T(8,128)(2,1)S(1)} %multiply_convert_fusion, bf16[448,256]{1,0:T(8,128)(2,1)S(1)} %all_gather.6), kind=kOutput, calls=%fused_computation | convolution fusion | flops 596705280 | bytes 4653056 | tf_op jit(solution)/shard_map/qd,ed->qe/dot_general | solution.py:51
  90.9 31.5 %reduce-scatter.11.cloned.1.call-done = bf16[112,512]{1,0:T(8,128)(2,1)} async-done(((bf16[112,4096]{1,0:T(8,128)(2,1)}), bf16[112,512]{1,0:T(8,128)(2,1)}) %reduce-scatter.11.cloned.1.call-update) | async-done | bytes 114704 | tf_op jit(solution)/shard_map/reduce_scatter | solution.py:59
  122.3 34.5 %reduce-scatter.5.cloned.1.call-done = bf16[256,2048]{1,0:T(8,128)(2,1)} async-done(((bf16[256,4096]{1,0:T(8,128)(2,1)}), bf16[256,2048]{1,0:T(8,128)(2,1)}) %reduce-scatter.5.cloned.1.call-update) | async-done | bytes 1048592 | tf_op jit(solution)/shard_map/reduce_scatter | solution.py:52
  (14 shorter events, 0.1 us)
Async XLA Ops:
  7.2 33.8 %copy-start = (bf16[1,4096,256]{2,1,0:T(8,128)(2,1)S(1)}, bf16[1,4096,256]{2,1,0:T(8,128)(2,1)}, u32[]{:S(2)}) copy-start(bf16[1,4096,256]{2,1,0:T(8,128)(2,1)} %param.8) | copy-start | bytes 6291460
  7.2 19.2 %copy-start.2 = (bf16[112,4096]{1,0:T(8,128)(2,1)S(1)}, bf16[112,4096]{1,0:T(8,128)(2,1)}, u32[]{:S(2)}) copy-start(bf16[112,4096]{1,0:T(8,128)(2,1)} %param.12) | copy-start | bytes 2752516
  7.2 57.2 %reduce-scatter.7.cloned.1.call-start = ((), (), s32[]{:S(2)}) async-start(), calls=%async_computation.5 | async-start | bytes 286720 | tf_op jit(solution)/shard_map/reduce_scatter | solution.py:42
  8.2 18.1 %copy-start.1 = (bf16[1,4096,256]{2,1,0:T(8,128)(2,1)S(1)}, bf16[1,4096,256]{2,1,0:T(8,128)(2,1)}, u32[]{:S(2)}) copy-start(bf16[1,4096,256]{2,1,0:T(8,128)(2,1)} %param.10) | copy-start | bytes 6291460
  10.7 30.3 %copy-start.3 = (bf16[1,256,4096]{2,1,0:T(8,128)(2,1)S(1)}, bf16[1,256,4096]{2,1,0:T(8,128)(2,1)}, u32[]{:S(2)}) copy-start(bf16[1,256,4096]{2,1,0:T(8,128)(2,1)} %param.7) | copy-start | bytes 6291460
  41.0 1.2 copy-start.4
  43.6 41.0 %reduce-scatter.9.cloned.1.call-start = ((), (), s32[]{:S(2)}) async-start(), calls=%async_computation.6 | async-start | bytes 286720 | tf_op jit(solution)/shard_map/reduce_scatter | solution.py:45
  44.6 77.7 %reduce-scatter.11.cloned.1.call-start = ((), (), s32[]{:S(2)}) async-start(), calls=%async_computation.7 | async-start | bytes 1032192 | tf_op jit(solution)/shard_map/reduce_scatter | solution.py:59
  88.5 68.4 %reduce-scatter.5.cloned.1.call-start = ((), (), s32[]{:S(2)}) async-start(), calls=%async_computation.4 | async-start | bytes 3145728 | tf_op jit(solution)/shard_map/reduce_scatter | solution.py:52
Sparse Core Ops, SparseCore 0:
  43.7 20.6 reduce-scatter.6
  66.8 17.7 reduce-scatter.8
  88.6 33.6 reduce-scatter.10
  125.0 31.7 reduce-scatter.4
where the time goes:
time: 164 us; the launch traced here: 163 us
  waiting for transfers between devices  102 us (62%)
  blocking collectives  29.8 us (18%)
  matrix products  16 us (10%)
  between operations  13.8 us (8%)
    reduce_scatter x1, waiting for transfers between devices, body(): lax.psum_scatter(input_term.astype(jnp.bfloat16), 'tensor', scatter_dimen...  34.5 us
    reduce_scatter x1, waiting for transfers between devices, body(): lax.psum_scatter(encoder_term.astype(jnp.bfloat16), ('tensor', 'section')...  31.5 us
    reduce_scatter x1, waiting for transfers between devices, body(): lax.psum_scatter(dkey_part.astype(jnp.bfloat16), 'seq', scatter_dimension...  19.7 us
    reduce_scatter x1, waiting for transfers between devices, body(): lax.psum_scatter(dvalue_part.astype(jnp.bfloat16), 'seq', scatter_dimensi...  16.5 us
    all_gather x1, blocking collectives, body(): lax.all_gather(key, 'seq', axis=0, tiled=True)  15.6 us
    all_gather x1, blocking collectives, body(): lax.all_gather(value, 'seq', axis=0, tiled=True)  14.2 us
    dot_general x1, matrix products, body(): jnp.einsum('kd,ed->ke', dvalue, wv_own, preferred_element_type=jnp.float32)  3.86 us
    dot_general x1, matrix products, body(): jnp.einsum('kd,ed->ke', dkey, wk_own, preferred_element_type=jnp.float32)  3.66 us
  transfers between devices with their start and end apart: 4, of which 4 were waited for; matrix products, arithmetic and copies ran while one was open for 4% of the time, Pallas kernels for 0%

commit v1 on v0

--- a/solution.py
+++ b/solution.py
@@ -5,6 +5,18 @@
 from jax.sharding import PartitionSpec as P
 
 masked_fill = -1e30
+
+
+def collect(x, axis, dim):
+    ways, here, step = (lax.axis_size(axis), lax.axis_index(axis), x.shape[dim])
+    line, have = (x, 1)
+    while have < ways:
+        line = jnp.concatenate(
+            [line, lax.ppermute(line, axis, [(d, (d - have) % ways) for d in range(ways)])],
+            axis=dim,
+        )
+        have = 2 * have
+    return jnp.roll(line, here * step, axis=dim)
 
 
 def body(dec_inputs, w_query, w_key, w_value, ctx_grad, encoded, enc_lengths):
@@ -19,10 +31,7 @@
     query = jnp.dot(inputs, wq_own, preferred_element_type=jnp.float32).astype(jnp.bfloat16)
     key = jnp.dot(encoded, wk_own, preferred_element_type=jnp.float32).astype(jnp.bfloat16)
     value = jnp.dot(encoded, wv_own, preferred_element_type=jnp.float32).astype(jnp.bfloat16)
-    key_all, value_all = (
-        lax.all_gather(key, "seq", axis=0, tiled=True),
-        lax.all_gather(value, "seq", axis=0, tiled=True),
-    )
+    key_all, value_all = (collect(key, "seq", 0), lax.all_gather(value, "seq", axis=0, tiled=True))
     limit = jnp.broadcast_to(enc_lengths[:, None], (blocks, kdev)).reshape(-1)
     slots = lax.broadcasted_iota(jnp.int32, (blocks, kdev), 1).reshape(-1)
     valid = (slots < limit)[None, :]

time: 164 us -> 157 us (0.957)
  blocking collectives: 29.8 us -> 15.1 us
  starting transfers between devices: 0.16 us -> 6.66 us
    all_gather x1 -> x0, blocking collectives: 15.6 us -> none  [body(): lax.all_gather(key, 'seq', axis=0, tiled=True)]
    ppermute x0 -> x2, starting transfers between devices: none -> 6.5 us  [collect(): lax.ppermute(line, axis, [(d, (d - have) % ways) for d in range(ways)])]
  transfers between devices with their start and end apart: 4 -> 6, of which waited for: 4 -> 5; matrix products, arithmetic and copies ran while one was open for 4% -> 5% of each run, Pallas kernels for 0% -> 0%
where the time goes in v1:
time: 157 us
  waiting for transfers between devices  103 us (66%)
  matrix products  16.9 us (11%)
  blocking collectives  15.1 us (10%)
  between operations  13.9 us (9%)
  starting transfers between devices  6.66 us (4%)
    reduce_scatter x1, waiting for transfers between devices, body(): lax.psum_scatter(input_term.astype(jnp.bfloat16), 'tensor', scatter_dimen...  34.5 us
    reduce_scatter x1, waiting for transfers between devices, body(): lax.psum_scatter(encoder_term.astype(jnp.bfloat16), ('tensor', 'section')...  31.4 us
    reduce_scatter x1, waiting for transfers between devices, body(): lax.psum_scatter(dkey_part.astype(jnp.bfloat16), 'seq', scatter_dimension...  19.7 us
    reduce_scatter x1, waiting for transfers between devices, body(): lax.psum_scatter(dvalue_part.astype(jnp.bfloat16), 'seq', scatter_dimensi...  16.5 us
    all_gather x1, blocking collectives, body(): lax.all_gather(value, 'seq', axis=0, tiled=True)  15.1 us
    ppermute x2, starting transfers between devices, collect(): lax.ppermute(line, axis, [(d, (d - have) % ways) for d in range(ways)])  6.5 us
    dot_general x1, matrix products, body(): jnp.einsum('kd,ed->ke', dvalue, wv_own, preferred_element_type=jnp.float32)  3.86 us
    dot_general x1, matrix products, body(): jnp.einsum('kd,ed->ke', dkey, wk_own, preferred_element_type=jnp.float32)  3.66 us
  transfers between devices with their start and end apart: 6, of which 5 were waited for; matrix products, arithmetic and copies ran while one was open for 5% of the time, Pallas kernels for 0%

profile of v1, /device:TPU:0, one launch (start us, length us, event | category | flops | bytes accessed | tf_op | source)
XLA Modules:
  0.0 156.6 jit_solution(4859808542436453612)
XLA Ops:
  7.2 2.5 %constant_dynamic-update-slice_fusion.5 = (bf16[896,256]{1,0:T(8,128)(2,1)S(1)}, bf16[112,256]{1,0:T(8,128)(2,1)S(1)}) fusion(bf16[112,4096]{1,0:T(8,128)(2,1)} %param.12, bf16[1,4096,256]{2,1,0:T(8,128)(2,1)} %param.9), kind=kOutput, calls=%fused_computation.39 | convolution fusion | flops 234909696 | bytes 3129344 | tf_op jit(solution)/shard_map/dot_general | solution.py:32
  9.7 5.1 %collective-permute-start = (bf16[112,256]{1,0:T(8,128)(2,1)S(1)}, bf16[112,256]{1,0:T(8,128)(2,1)S(1)}, u32[]{:S(2)}, u32[]{:S(2)}) collective-permute-start(bf16[112,256]{1,0:T(8,128)(2,1)S(1)} %get-tuple-element.3), channel_id=1, source_target_pairs={{0,24},{8,0},{16,8},{24,16},{1,25},{9,1},{17,9},{25,17},{2,26},{10... | collective-permute-start | bytes 172040 | tf_op jit(solution)/shard_map/ppermute | solution.py:15
  14.8 0.5 fusion.21
  15.4 0.7 fusion.13
  16.1 0.1 iota_compare_fusion
  16.2 0.5 collective-permute-done
  16.7 1.4 collective-permute-start.1
  18.1 15.1 %all_gather.3 = bf16[448,256]{1,0:T(8,128)(2,1)} all-gather(bf16[112,256]{1,0:T(8,128)(2,1)S(1)} %fusion.21), channel_id=1, replica_groups=mesh['seq'=4,'tensor'=2,'section'=4] {'seq'}, dimensions={0}, use_global_device_ids=true | all-gather | bytes 286720 | tf_op jit(solution)/shard_map/all_gather | solution.py:34
  33.2 0.1 lt.23
  33.3 0.8 constant_dynamic-update-slice_fusion.2
  34.1 0.3 fusion.36
  34.4 0.1 fusion.25
  34.6 1.2 multiply_reduce_fusion
  35.8 0.2 multiply_convert_fusion
  36.0 0.9 convolution_convert_fusion.2
  36.9 0.0 reduce-scatter.9.cloned.1.call-start
  37.0 1.0 convolution_convert_fusion.1
  38.0 19.7 %reduce-scatter.7.cloned.1.call-done = bf16[112,256]{1,0:T(8,128)(2,1)} async-done(((bf16[448,256]{1,0:T(8,128)(2,1)}), bf16[112,256]{1,0:T(8,128)(2,1)}) %reduce-scatter.7.cloned.1.call-update) | async-done | bytes 57360 | tf_op jit(solution)/shard_map/reduce_scatter | solution.py:51
  57.7 3.7 %fusion.4 = f32[112,4096]{1,0:T(8,128)} fusion(bf16[112,256]{1,0:T(8,128)(2,1)} %reduce-scatter.7.cloned.1.call-done, bf16[1,4096,256]{2,1,0:T(8,128)(2,1)} %param.9), kind=kOutput, calls=%fused_computation.6 | convolution fusion | flops 234881024 | bytes 3989504 | tf_op jit(solution)/shard_map/kd,ed->ke/dot_general | solution.py:64
  61.3 16.5 %reduce-scatter.9.cloned.1.call-done = bf16[112,256]{1,0:T(8,128)(2,1)} async-done(((bf16[448,256]{1,0:T(8,128)(2,1)}), bf16[112,256]{1,0:T(8,128)(2,1)}) %reduce-scatter.9.cloned.1.call-update) | async-done | bytes 57360 | tf_op jit(solution)/shard_map/reduce_scatter | solution.py:54
  77.8 3.9 %fusion = bf16[112,4096]{1,0:T(8,128)(2,1)} fusion(f32[112,4096]{1,0:T(8,128)} %fusion.4, bf16[112,256]{1,0:T(8,128)(2,1)} %reduce-scatter.9.cloned.1.call-done, bf16[1,4096,256]{2,1,0:T(8,128)(2,1)} %param.10), kind=kOutput, calls=%fused_computation.2 | convolution fusion | flops 235798528 | bytes 4907008 | tf_op jit(solution)/shard_map/kd,ed->ke/dot_general | solution.py:65
  81.8 2.3 %convolution_convert_fusion = bf16[256,4096]{1,0:T(8,128)(2,1)} fusion(bf16[1,4096,256]{2,1,0:T(8,128)(2,1)S(1)} %copy-done, bf16[256,448]{0,1:T(8,128)(2,1)S(1)} %multiply_convert_fusion, bf16[896,256]{1,0:T(8,128)(2,1)S(1)} %constant_dynamic-update-slice_fusion, s32[]{:T(128)S(6)} %select_n.21), kind=kOutput, calls=%fused_computation | convolution fusion | flops 596705280 | bytes 4653060 | tf_op jit(solution)/shard_map/qd,ed->qe/dot_general | solution.py:60
  84.1 31.4 %reduce-scatter.11.cloned.1.call-done = bf16[112,512]{1,0:T(8,128)(2,1)} async-done(((bf16[112,4096]{1,0:T(8,128)(2,1)}), bf16[112,512]{1,0:T(8,128)(2,1)}) %reduce-scatter.11.cloned.1.call-update) | async-done | bytes 114704 | tf_op jit(solution)/shard_map/reduce_scatter | solution.py:68
  115.5 34.5 %reduce-scatter.5.cloned.1.call-done = bf16[256,2048]{1,0:T(8,128)(2,1)} async-done(((bf16[256,4096]{1,0:T(8,128)(2,1)}), bf16[256,2048]{1,0:T(8,128)(2,1)}) %reduce-scatter.5.cloned.1.call-update) | async-done | bytes 1048592 | tf_op jit(solution)/shard_map/reduce_scatter | solution.py:61
  (27 shorter events, 0.3 us)
Async XLA Ops:
  7.2 8.2 %copy-start = (bf16[1,4096,256]{2,1,0:T(8,128)(2,1)S(1)}, bf16[1,4096,256]{2,1,0:T(8,128)(2,1)}, u32[]{:S(2)}) copy-start(bf16[1,4096,256]{2,1,0:T(8,128)(2,1)} %param.8) | copy-start | bytes 6291460
  7.2 7.7 %copy-start.2 = (bf16[112,4096]{1,0:T(8,128)(2,1)S(1)}, bf16[112,4096]{1,0:T(8,128)(2,1)}, u32[]{:S(2)}) copy-start(bf16[112,4096]{1,0:T(8,128)(2,1)} %param.12) | copy-start | bytes 2752516
  7.2 50.5 %reduce-scatter.7.cloned.1.call-start = ((), (), s32[]{:S(2)}) async-start(), calls=%async_computation.5 | async-start | bytes 286720 | tf_op jit(solution)/shard_map/reduce_scatter | solution.py:51
  7.2 7.6 %copy-start.1 = (bf16[1,4096,256]{2,1,0:T(8,128)(2,1)S(1)}, bf16[1,4096,256]{2,1,0:T(8,128)(2,1)}, u32[]{:S(2)}) copy-start(bf16[1,4096,256]{2,1,0:T(8,128)(2,1)} %param.10) | copy-start | bytes 6291460
  9.7 7.0 %copy-start.3 = (bf16[112,256]{1,0:T(8,128)(2,1)}, bf16[112,256]{1,0:T(8,128)(2,1)S(1)}, u32[]{:S(2)}) copy-start(bf16[112,256]{1,0:T(8,128)(2,1)S(1)} %get-tuple-element.3) | copy-start | bytes 172036
  9.7 5.6 %copy-start.4 = (bf16[1,256,4096]{2,1,0:T(8,128)(2,1)S(1)}, bf16[1,256,4096]{2,1,0:T(8,128)(2,1)}, u32[]{:S(2)}) copy-start(bf16[1,256,4096]{2,1,0:T(8,128)(2,1)} %param.7) | copy-start | bytes 6291460
  9.7 6.9 %collective-permute-start = (bf16[112,256]{1,0:T(8,128)(2,1)S(1)}, bf16[112,256]{1,0:T(8,128)(2,1)S(1)}, u32[]{:S(2)}, u32[]{:S(2)}) collective-permute-start(bf16[112,256]{1,0:T(8,128)(2,1)S(1)} %get-tuple-element.3), channel_id=1, source_target_pairs={{0,24},{8,0},{16,8},{24,16},{1,25},{9,1},{17,9},{25,17},{2,26},{10... | collective-permute-start | bytes 172040 | tf_op jit(solution)/shard_map/ppermute | solution.py:15
  15.4 0.7 copy-start.6
  16.1 18.5 %copy-start.5 = (bf16[1,256,256]{2,1,0:T(8,128)(2,1)S(1)}, bf16[1,256,256]{2,1,0:T(8,128)(2,1)}, u32[]{:S(2)}) copy-start(bf16[1,256,256]{2,1,0:T(8,128)(2,1)} %param.11) | copy-start | bytes 393220
  16.7 16.6 %collective-permute-start.1 = (bf16[224,256]{1,0:T(8,128)(2,1)S(1)}, bf16[224,256]{1,0:T(8,128)(2,1)S(1)}, u32[]{:S(2)}, u32[]{:S(2)}) collective-permute-start(bf16[224,256]{1,0:T(8,128)(2,1)S(1)} %pad_maximum_fusion), channel_id=1, source_target_pairs={{0,16},{8,24},{16,0},{24,8},{1,17},{9,25},{17,1},{25,9},{2,18},{10... | collective-permute-start | bytes 344072 | tf_op jit(solution)/shard_map/ppermute | solution.py:15
  36.9 40.9 %reduce-scatter.9.cloned.1.call-start = ((), (), s32[]{:S(2)}) async-start(), calls=%async_computation.6 | async-start | bytes 286720 | tf_op jit(solution)/shard_map/reduce_scatter | solution.py:54
  38.0 77.6 %reduce-scatter.11.cloned.1.call-start = ((), (), s32[]{:S(2)}) async-start(), calls=%async_computation.7 | async-start | bytes 1032192 | tf_op jit(solution)/shard_map/reduce_scatter | solution.py:68
  81.7 68.4 %reduce-scatter.5.cloned.1.call-start = ((), (), s32[]{:S(2)}) async-start(), calls=%async_computation.4 | async-start | bytes 3145728 | tf_op jit(solution)/shard_map/reduce_scatter | solution.py:61
Sparse Core Ops, SparseCore 0:
  37.1 20.5 reduce-scatter.6
  60.0 17.7 reduce-scatter.8
  81.8 33.6 reduce-scatter.10
  118.2 31.8 reduce-scatter.4
